TPU v7x, 32 devices: a whole 2x2x4 slice. The times are simulated.
32 devices in a mesh: kvh: 2 (over x), ctx: 16 (over z, y, core).
Axes of the slice: x: 2, y: 2, z: 4, core: 2. Of those that a mesh axis runs over, the one named last changes fastest.
Arguments:
- queries: bfloat16 [512, 32, 128], P('ctx', 'kvh'), parts along dimension 1, may hold values from -6 to 6
- cache_keys: bfloat16 [16384, 256], P('ctx', 'kvh'), parts along dimension 1, may hold values from -6 to 6
- cache_values: bfloat16 [16384, 256], P('ctx', 'kvh'), parts along dimension 1, may hold values from -6 to 6
- span_offset: int32 [1], replicated, may hold values from 0 to 8191
- positions: int32 [512], replicated, may hold values from 0 to 8191
Outputs:
- attended: bfloat16 [512, 32, 128], P('ctx', 'kvh'), parts along dimension 1
There are 2 independent parts, one for each index of `kvh`. A program takes and returns all parts, laid end to end along the dimension named above; an argument that names none is the same for every part. Nothing has to cross between parts.
All inputs are finite; a program needn't handle non-finite values.
Results may differ from a plain program's by a relative error of at most 0.0029.
Values may be sent and summed in bfloat16 or wider, within the bound.
No kernel may reach another device: no remote copies, remote signals or barrier semaphores. Data moves between devices by JAX's collectives and lax.ppermute only.
A program may use at most 64 MiB of HBM per device.

v0:
```python
import jax
import jax.numpy as jnp
from jax import lax
from jax.sharding import PartitionSpec as P

masked_floor = -1e30


def local(queries, cache_keys, cache_values, span_offset, positions):
    gathered = lax.all_gather(queries, "ctx", axis=0, tiled=True)
    token_count, head_count, head_width = gathered.shape
    row_count = token_count * head_count
    shard_keys = cache_keys.shape[0]
    key_start = lax.axis_index("ctx") * shard_keys
    key_position = key_start + lax.iota(jnp.int32, shard_keys)
    row_limit = jnp.repeat(span_offset[0] + positions, head_count)
    row_block = 512
    block_count = row_count // row_block
    query_blocks = gathered.reshape(block_count, row_block, head_width)
    limit_blocks = row_limit.reshape(block_count, row_block)
    score_scale = head_width ** (-0.5)

    def shard_partial(inputs):
        query_block, limit_block = inputs
        scores = (
            lax.dot_general(
                query_block,
                cache_keys,
                (((1,), (1,)), ((), ())),
                preferred_element_type=jnp.float32,
            )
            * score_scale
        )
        visible = key_position[None, :] <= limit_block[:, None]
        shard_max = jnp.max(jnp.where(visible, scores, masked_floor), axis=1)
        weights = jnp.where(visible, jnp.exp(scores - shard_max[:, None]), 0.0).astype(jnp.bfloat16)
        shard_den = jnp.sum(weights.astype(jnp.float32), axis=1)
        shard_num = jnp.dot(weights, cache_values, preferred_element_type=jnp.float32)
        return (shard_num, shard_max, shard_den)

    numerator, local_max, denominator = lax.map(shard_partial, (query_blocks, limit_blocks))
    numerator = numerator.reshape(token_count, head_count * head_width)
    local_max = local_max.reshape(token_count, head_count)
    denominator = denominator.reshape(token_count, head_count)
    got_num, got_max, got_den = (
        lax.all_to_all(numerator[None], "ctx", split_axis=1, concat_axis=0, tiled=True),
        lax.all_to_all(local_max[None], "ctx", split_axis=1, concat_axis=0, tiled=True),
        lax.all_to_all(denominator[None], "ctx", split_axis=1, concat_axis=0, tiled=True),
    )
    row_top = jnp.max(got_max, axis=0)
    factor = jnp.exp(got_max - row_top[None])
    sources, own_tokens = (got_max.shape[0], got_max.shape[1])
    num_sum = jnp.sum(
        got_num.reshape(sources, own_tokens, head_count, head_width) * factor[:, :, :, None], axis=0
    )
    den_sum = jnp.sum(got_den * factor, axis=0)
    attended = num_sum / den_sum[:, :, None]
    return attended.astype(jnp.bfloat16)


def solution(mesh):
    in_specs = (P("ctx", "kvh", None), P("ctx", "kvh"), P("ctx", "kvh"), P(), P())
    out_specs = P("ctx", "kvh", None)
    return jax.shard_map(local, mesh=mesh, in_specs=in_specs, out_specs=out_specs, check_vma=False)
```

profile of v0, /device:TPU:13, one launch (start us, length us, event | category | flops | bytes accessed | tf_op | source)
XLA Modules:
  0.0 250.9 jit_solution(5904179462942185829)
XLA Ops:
  9.0 41.5 %all-gather.2.cloned.1.call-done = bf16[512,16,128]{2,1,0:T(8,128)(2,1)} async-done(((bf16[32,16,128]{2,1,0:T(8,128)(2,1)}), bf16[512,16,128]{2,1,0:T(8,128)(2,1)}) %all-gather.2.cloned.1.call-update) | async-done | bytes 2097168 | tf_op jit(solution)/shard_map/all_gather | solution.py:10
  50.5 59.1 %while.15 = (s32[]{:T(128)}, f32[16,512,128]{2,1,0:T(8,128)}, f32[16,512]{1,0:T(8,128)S(1)}, f32[16,512]{1,0:T(8,128)S(1)}, s32[16,512]{1,0:T(8,128)S(1)}, /*ind...) while((s32[]{:T(128)}, f32[16,512,128]{2,1,0:T(8,128)}, ...), condition=%wide.region_3.4_spmd.clone, body=%wide.region_0.3_spmd.clone.sunk | while | flops 274202624 | bytes 8292521 | solution.py:41
  50.5 1.6 fusion.22
  52.1 0.7 convert_reduce_fusion.2
  53.1 1.1 fusion.23
  54.2 1.6 fusion.22
  56.7 1.1 fusion.23
  57.9 1.6 fusion.22
  59.5 0.7 convert_reduce_fusion.2
  60.4 1.1 fusion.23
  61.6 1.6 fusion.22
  64.1 1.2 fusion.23
  65.3 1.6 fusion.22
  67.8 1.2 fusion.23
  69.0 1.6 fusion.22
  71.5 1.2 fusion.23
  72.7 1.6 fusion.22
  75.2 1.1 fusion.23
  76.4 1.6 fusion.22
  78.0 0.7 convert_reduce_fusion.2
  78.9 1.2 fusion.23
  80.1 1.6 fusion.22
  82.6 1.2 fusion.23
  83.8 1.6 fusion.22
  86.3 1.1 fusion.23
  87.5 1.6 fusion.22
  90.0 1.1 fusion.23
  91.1 1.6 fusion.22
  93.7 1.2 fusion.23
  94.8 1.6 fusion.22
  97.4 1.2 fusion.23
  98.5 1.6 fusion.22
  101.1 1.2 fusion.23
  102.2 1.6 fusion.22
  104.8 1.1 fusion.23
  105.9 1.6 fusion.22
  108.5 1.1 fusion.23
  110.2 1.2 reduce.1
  111.4 0.8 reshape.55
  112.2 5.7 %all-to-all-start.2 = ((f32[16,1,512]{2,1,0:T(1,128)}), f32[16,1,512]{2,1,0:T(1,128)S(1)}, u32[]{:S(2)}, u32[]{:S(2)}) async-start(f32[16,1,512]{2,1,0:T(1,128)} %reshape.55), calls=%async_computation.2 | async-start | bytes 65536 | tf_op jit(solution)/shard_map/all_to_all | solution.py:48
  118.1 1.2 reduce.3
  119.4 2.7 %all-to-all-done.2 = f32[16,1,512]{2,1,0:T(1,128)S(1)} async-done(((f32[16,1,512]{2,1,0:T(1,128)}), f32[16,1,512]{2,1,0:T(1,128)S(1)}, u32[]{:S(2)}, u32[]{:S(2)}) %all-to-all-start.2) | async-done | bytes 32800 | tf_op jit(solution)/shard_map/all_to_all | solution.py:48
  122.1 9.2 %all_to_all.36 = f32[16,1,512]{2,1,0:T(1,128)S(1)} all-to-all(f32[16,1,512]{2,1,0:T(1,128)S(1)} %reshape.53), channel_id=1, replica_groups=mesh['kvh'=2,'ctx'=16] {'ctx'}, dimensions={0} | all-to-all | bytes 65536 | tf_op jit(solution)/shard_map/all_to_all | solution.py:47
  131.3 6.8 %all-to-all-start = ((f32[1,512,2048]{2,0,1:T(1,128)}), f32[1,512,2048]{2,0,1:T(1,128)}, u32[]{:S(2)}, u32[]{:S(2)}) async-start(f32[1,512,2048]{2,0,1:T(1,128)} %bitcast.51), calls=%async_computation | async-start | bytes 8388608 | tf_op jit(solution)/shard_map/all_to_all | solution.py:46
  140.6 90.1 %all-to-all-done = f32[1,512,2048]{2,0,1:T(1,128)} async-done(((f32[1,512,2048]{2,0,1:T(1,128)}), f32[1,512,2048]{2,0,1:T(1,128)}, u32[]{:S(2)}, u32[]{:S(2)}) %all-to-all-start) | async-done | bytes 4194336 | tf_op jit(solution)/shard_map/all_to_all | solution.py:46
  230.7 2.5 %mul.33 = f32[16,32,16,128]{3,2,1,0:T(8,128)} broadcast(f32[16,32,16]{2,1,0:T(8,128)S(1)} %get-tuple-element.99), dimensions={0,1,2} | broadcast | bytes 4227072 | tf_op jit(solution)/shard_map/mul | solution.py:54
  233.2 10.0 %multiply_reduce_fusion = f32[32,2048]{1,0:T(8,128)S(1)} fusion(f32[1,16,32,2048]{3,0,2,1:T(1,128)} %bitcast.3, f32[1,16,32,2048]{3,0,2,1:T(1,128)} %bitcast.50), kind=kLoop, calls=%fused_computation.14 | loop fusion | flops 2031616 | bytes 8650752 | tf_op jit(solution)/shard_map/reduce_sum | solution.py:53
  243.3 0.8 fusion.9
  (129 shorter events, 18.0 us)
Async XLA Ops:
  6.5 44.0 %all-gather.2.cloned.1.call-start = ((), (), s32[]{:S(2)}) async-start(), calls=%async_computation.3 | async-start | bytes 2228224 | tf_op jit(solution)/shard_map/all_gather | solution.py:10
  52.1 1.0 copy-start
  55.8 1.0 copy-start
  59.5 1.0 copy-start
  63.2 1.0 copy-start
  66.9 1.0 copy-start
  70.6 1.0 copy-start
  74.3 1.0 copy-start
  77.9 1.0 copy-start
  81.6 1.0 copy-start
  85.3 1.0 copy-start
  89.0 1.0 copy-start
  92.7 1.0 copy-start
  96.4 1.0 copy-start
  100.1 1.0 copy-start
  103.8 1.0 copy-start
  107.5 1.0 copy-start
  112.2 9.9 %all-to-all-start.2 = ((f32[16,1,512]{2,1,0:T(1,128)}), f32[16,1,512]{2,1,0:T(1,128)S(1)}, u32[]{:S(2)}, u32[]{:S(2)}) async-start(f32[16,1,512]{2,1,0:T(1,128)} %reshape.55), calls=%async_computation.2 | async-start | bytes 65536 | tf_op jit(solution)/shard_map/all_to_all | solution.py:48
  131.3 99.3 %all-to-all-start = ((f32[1,512,2048]{2,0,1:T(1,128)}), f32[1,512,2048]{2,0,1:T(1,128)}, u32[]{:S(2)}, u32[]{:S(2)}) async-start(f32[1,512,2048]{2,0,1:T(1,128)} %bitcast.51), calls=%async_computation | async-start | bytes 8388608 | tf_op jit(solution)/shard_map/all_to_all | solution.py:46
Sparse Core Ops, SparseCore 0:
  9.5 40.9 all-gather.1
where the time goes:
time: 252 us; the launch traced here: 251 us
  waiting for transfers between devices  135 us (54%)
  matrix products  43.6 us (17%)
  other arithmetic  26.8 us (11%)
  between operations  14.2 us (6%)
  starting transfers between devices  12.6 us (5%)
  blocking collectives  9.19 us (4%)
  local copies, waits for them, and re-layouts  9.16 us (4%)
    all_to_all x1, waiting for transfers between devices, local(): lax.all_to_all(numerator[None], 'ctx', split_axis=1, concat_axis=0, tiled...  90.1 us
    all_gather x1, waiting for transfers between devices, local(): gathered = lax.all_gather(queries, 'ctx', axis=0, tiled=True)  41.5 us
    dot_general x16, matrix products, shard_partial(): lax.dot_general(query_block, cache_keys, (((1,), (1,)), ((), ())), prefer...  25.2 us
    dot_general x16, matrix products, shard_partial(): jnp.dot(weights, cache_values, preferred_element_type=jnp.float32)  18.4 us
    reduce_sum x16, other arithmetic, shard_partial(): shard_den = jnp.sum(weights.astype(jnp.float32), axis=1)  11.4 us
    reduce_sum x1, other arithmetic, local(): jnp.sum(got_num.reshape(sources, own_tokens, head_count, head_width) * fa...  10 us
    all_to_all x1, blocking collectives, local(): lax.all_to_all(local_max[None], 'ctx', split_axis=1, concat_axis=0, tiled...  9.19 us
    all_to_all x1, starting transfers between devices, local(): lax.all_to_all(numerator[None], 'ctx', split_axis=1, concat_axis=0, tiled...  6.85 us
  transfers between devices with their start and end apart: 3, of which 3 were waited for; matrix products, arithmetic and copies ran while one was open for 2% of the time, Pallas kernels for 0%

commit v1 on v0

--- a/solution.py
+++ b/solution.py
@@ -4,6 +4,12 @@
 from jax.sharding import PartitionSpec as P
 
 masked_floor = -1e30
+
+
+def exchange_blocks(block, axis, split, join):
+    pieces = jnp.split(block, lax.axis_size(axis), axis=split)
+    received = lax.all_to_all(jnp.stack(pieces), axis, 0, 0)
+    return jnp.concatenate(received, axis=join)
 
 
 def local(queries, cache_keys, cache_values, span_offset, positions):
@@ -43,7 +49,7 @@
     local_max = local_max.reshape(token_count, head_count)
     denominator = denominator.reshape(token_count, head_count)
     got_num, got_max, got_den = (
-        lax.all_to_all(numerator[None], "ctx", split_axis=1, concat_axis=0, tiled=True),
+        exchange_blocks(numerator[None], "ctx", 1, 0),
         lax.all_to_all(local_max[None], "ctx", split_axis=1, concat_axis=0, tiled=True),
         lax.all_to_all(denominator[None], "ctx", split_axis=1, concat_axis=0, tiled=True),
     )

time: 252 us -> 273 us (1.083)
  local copies, waits for them, and re-layouts: 9.16 us -> 44.8 us
  blocking collectives: 9.19 us -> 0 us
  waiting for transfers between devices: 135 us -> 127 us
  starting transfers between devices: 12.6 us -> 18.4 us
  other arithmetic: 26.8 us -> 21.4 us
    unnamed x6 -> x21, local copies, waits for them, and re-layouts: 2.42 us -> 28.3 us
    all_to_all x1 -> x0, blocking collectives: 9.19 us -> none  [local(): lax.all_to_all(local_max[None], 'ctx', split_axis=1, concat_axis=0, tiled...]
    all_to_all x1 -> x2, waiting for transfers between devices: 90.1 us -> 82.7 us  [the longest x1 82.3 us: exchange_blocks(): received = lax.all_to_all(jnp.stack(pieces), axis, 0, 0)]
    another operation x0 -> x2, local copies, waits for them, and re-layouts: none -> 6.56 us  [the longest x1 4.88 us: local(): numerator[None]]
    reduce_sum x1, other arithmetic: 10 us -> 4.05 us  [local(): jnp.sum(got_num.reshape(sources, own_tokens, head_count, head_width) * fa...]
    all_to_all x1 -> x2, starting transfers between devices: 6.85 us -> 12.6 us  [the longest x1 6.85 us: exchange_blocks(): received = lax.all_to_all(jnp.stack(pieces), axis, 0, 0)]
    mul x1 -> x2, local copies, waits for them, and re-layouts: 2.53 us -> 7.5 us  [local(): got_num.reshape(sources, own_tokens, head_count, head_width)]
  transfers between devices with their start and end apart: 3 -> 4, of which waited for: 3 -> 4; matrix products, arithmetic and copies ran while one was open for 2% -> 6% of each run, Pallas kernels for 0% -> 0%
where the time goes in v1:
time: 273 us; the launch traced here: 271 us
  waiting for transfers between devices  127 us (47%)
  local copies, waits for them, and re-layouts  44.8 us (16%)
  matrix products  44.1 us (16%)
  other arithmetic  21.4 us (8%)
  starting transfers between devices  18.4 us (7%)
  between operations  14.2 us (5%)
    all_to_all x1, waiting for transfers between devices, exchange_blocks(): received = lax.all_to_all(jnp.stack(pieces), axis, 0, 0)  82.3 us
    all_gather x1, waiting for transfers between devices, local(): gathered = lax.all_gather(queries, 'ctx', axis=0, tiled=True)  41.5 us
    unnamed x21, local copies, waits for them, and re-layouts  28.3 us
    dot_general x16, matrix products, shard_partial(): lax.dot_general(query_block, cache_keys, (((1,), (1,)), ((), ())), prefer...  25.6 us
    dot_general x16, matrix products, shard_partial(): jnp.dot(weights, cache_values, preferred_element_type=jnp.float32)  18.5 us
    reduce_sum x16, other arithmetic, shard_partial(): shard_den = jnp.sum(weights.astype(jnp.float32), axis=1)  11.5 us
    mul x2, local copies, waits for them, and re-layouts, local(): got_num.reshape(sources, own_tokens, head_count, head_width)  7.5 us
    all_to_all x1, starting transfers between devices, exchange_blocks(): received = lax.all_to_all(jnp.stack(pieces), axis, 0, 0)  6.85 us
  transfers between devices with their start and end apart: 4, of which 4 were waited for; matrix products, arithmetic and copies ran while one was open for 6% of the time, Pallas kernels for 0%

profile of v1, /device:TPU:13, one launch (start us, length us, event | category | flops | bytes accessed | tf_op | source)
XLA Modules:
  0.0 271.2 jit_solution(17165158210022789043)
XLA Ops:
  9.0 41.5 %all-gather.2.cloned.1.call-done = bf16[512,16,128]{2,1,0:T(8,128)(2,1)} async-done(((bf16[32,16,128]{2,1,0:T(8,128)(2,1)}), bf16[512,16,128]{2,1,0:T(8,128)(2,1)}) %all-gather.2.cloned.1.call-update) | async-done | bytes 2097168 | tf_op jit(solution)/shard_map/all_gather | solution.py:16
  50.5 58.4 %while.15 = (s32[]{:T(128)}, f32[16,512,128]{2,1,0:T(8,128)}, f32[16,512]{1,0:T(8,128)S(1)}, f32[16,512]{1,0:T(8,128)S(1)}, s32[16,512]{1,0:T(8,128)S(1)}, /*ind...) while((s32[]{:T(128)}, f32[16,512,128]{2,1,0:T(8,128)}, ...), condition=%wide.region_3.4_spmd.clone, body=%wide.region_0.3_spmd.clone.sunk | while | flops 274202624 | bytes 8293529 | solution.py:47
  50.6 1.6 fusion.38
  54.2 1.6 fusion.38
  57.8 1.6 fusion.38
  61.5 1.6 fusion.38
  63.8 1.2 fusion.39
  65.2 1.6 fusion.38
  68.8 1.6 fusion.38
  71.1 1.2 fusion.39
  72.5 1.6 fusion.38
  76.1 1.6 fusion.38
  79.8 1.6 fusion.38
  83.4 1.6 fusion.38
  87.1 1.6 fusion.38
  90.7 1.6 fusion.38
  94.4 1.6 fusion.38
  98.0 1.6 fusion.38
  101.7 1.6 fusion.38
  105.3 1.6 fusion.38
  107.6 1.2 fusion.39
  108.9 4.9 %broadcast_in_dim_reshape.9 = f32[1,512,2048]{2,1,0:T(8,128)} reshape(f32[16,512,128]{2,1,0:T(8,128)} %get-tuple-element.54) | data formatting | bytes 8388608 | tf_op jit(solution)/shard_map/broadcast_in_dim;reshape | solution.py:52
  113.8 1.7 fusion.25
  115.5 1.7 fusion.24
  117.1 1.7 fusion.23
  118.8 1.7 fusion.22
  120.5 1.7 fusion.21
  122.2 1.7 fusion.20
  123.9 1.7 fusion.19
  125.6 1.7 fusion.18
  127.2 1.7 fusion.17
  128.9 1.7 fusion.16
  130.6 1.7 fusion.15
  132.3 1.7 fusion.14
  134.0 1.7 fusion.13
  135.6 1.7 fusion.12
  138.0 1.3 reduce.3
  140.1 5.7 %all-to-all-start.1 = ((f32[16,1,512]{2,1,0:T(1,128)}), f32[16,1,512]{2,1,0:T(1,128)S(1)}, u32[]{:S(2)}, u32[]{:S(2)}) async-start(f32[16,1,512]{2,1,0:T(1,128)} %reshape.31), calls=%async_computation.1 | async-start | bytes 65536 | tf_op jit(solution)/shard_map/all_to_all | solution.py:53
  145.8 1.7 fusion.11
  147.6 1.3 reduce.1
  150.0 5.9 %all-to-all-start.2 = ((f32[16,1,512]{2,1,0:T(1,128)}), f32[16,1,512]{2,1,0:T(1,128)S(1)}, u32[]{:S(2)}, u32[]{:S(2)}) async-start(f32[16,1,512]{2,1,0:T(1,128)} %reshape.33), calls=%async_computation.2 | async-start | bytes 65536 | tf_op jit(solution)/shard_map/all_to_all | solution.py:54
  155.9 1.7 fusion.10
  157.6 2.5 all-to-all-done.2
  160.1 6.9 %all-to-all-start = ((f32[16,1,32,2048]{3,2,1,0:T(8,128)}), f32[16,1,32,2048]{3,2,1,0:T(8,128)}, u32[]{:S(2)}, u32[]{:S(2)}) async-start(f32[16,1,32,2048]{3,2,1,0:T(8,128)} %fusion.10), calls=%async_computation | async-start | bytes 8388608 | tf_op jit(solution)/shard_map/all_to_all | solution.py:11
  169.6 2.6 mul.24
  172.2 4.9 %mul.25 = f32[16,1,32,2048]{3,2,1,0:T(8,128)} reshape(f32[16,32,16,128]{3,2,1,0:T(8,128)} %mul.24) | data formatting | bytes 8388608 | tf_op jit(solution)/shard_map/mul | solution.py:60
  177.1 82.3 %all-to-all-done = f32[16,1,32,2048]{3,2,1,0:T(8,128)} async-done(((f32[16,1,32,2048]{3,2,1,0:T(8,128)}), f32[16,1,32,2048]{3,2,1,0:T(8,128)}, u32[]{:S(2)}, u32[]{:S(2)}) %all-to-all-start) | async-done | bytes 4194336 | tf_op jit(solution)/shard_map/all_to_all | solution.py:11
  259.5 4.1 %multiply_reduce_fusion = f32[32,2048]{1,0:T(8,128)S(1)} fusion(f32[16,1,32,2048]{3,2,1,0:T(8,128)} %all-to-all-done, f32[16,1,32,2048]{3,2,1,0:T(8,128)} %mul.25), kind=kLoop, calls=%fused_computation.14 | loop fusion | flops 2031616 | bytes 8650752 | tf_op jit(solution)/shard_map/reduce_sum | solution.py:59
  (148 shorter events, 36.2 us)
Async XLA Ops:
  6.5 44.0 %all-gather.2.cloned.1.call-start = ((), (), s32[]{:S(2)}) async-start(), calls=%async_computation.3 | async-start | bytes 2228224 | tf_op jit(solution)/shard_map/all_gather | solution.py:16
  50.5 2.3 copy-start
  54.1 2.4 copy-start
  57.8 2.4 copy-start
  61.5 2.4 copy-start
  65.1 2.4 copy-start
  68.8 2.4 copy-start
  72.4 2.4 copy-start
  76.1 2.4 copy-start
  79.7 2.4 copy-start
  83.4 2.4 copy-start
  87.0 2.4 copy-start
  90.7 2.4 copy-start
  94.3 2.4 copy-start
  98.0 2.4 copy-start
  101.6 2.4 copy-start
  105.3 2.4 copy-start
  140.1 9.9 %all-to-all-start.1 = ((f32[16,1,512]{2,1,0:T(1,128)}), f32[16,1,512]{2,1,0:T(1,128)S(1)}, u32[]{:S(2)}, u32[]{:S(2)}) async-start(f32[16,1,512]{2,1,0:T(1,128)} %reshape.31), calls=%async_computation.1 | async-start | bytes 65536 | tf_op jit(solution)/shard_map/all_to_all | solution.py:53
  150.0 10.1 %all-to-all-start.2 = ((f32[16,1,512]{2,1,0:T(1,128)}), f32[16,1,512]{2,1,0:T(1,128)S(1)}, u32[]{:S(2)}, u32[]{:S(2)}) async-start(f32[16,1,512]{2,1,0:T(1,128)} %reshape.33), calls=%async_computation.2 | async-start | bytes 65536 | tf_op jit(solution)/shard_map/all_to_all | solution.py:54
  160.1 99.3 %all-to-all-start = ((f32[16,1,32,2048]{3,2,1,0:T(8,128)}), f32[16,1,32,2048]{3,2,1,0:T(8,128)}, u32[]{:S(2)}, u32[]{:S(2)}) async-start(f32[16,1,32,2048]{3,2,1,0:T(8,128)} %fusion.10), calls=%async_computation | async-start | bytes 8388608 | tf_op jit(solution)/shard_map/all_to_all | solution.py:11
Sparse Core Ops, SparseCore 0:
  9.5 40.9 all-gather.1
